TPU v7x, 128 devices: a whole 4x4x4 slice. The times are simulated.
128 devices in a mesh: rows: 8 (over z, core), cols: 16 (over y, x).
Axes of the slice: x: 4, y: 4, z: 4, core: 2. Of those that a mesh axis runs over, the one named last changes fastest.
Arguments:
- pivot_rhs: float32 [4, 4096, 1024], P(None, 'cols'), may hold values from -6 to 6
- bound_sol: bfloat16 [16384, 1024], P('rows'), may hold values from -6 to 6
- border_tiles: bfloat16 [16384, 4, 4096], P('rows', None, 'cols'), may hold values from -0.046875 to 0.046875
- lower_tiles: bfloat16 [6, 4096, 4096], P(None, 'rows', 'cols'), may hold values from -0.09375 to 0.09375
- inverse_diag: bfloat16 [4, 4096, 4096], P(None, 'cols', 'rows'), may hold values from -0.09375 to 0.09375
- owner_map: int32 [128, 128, 1], P(('rows', 'cols')), may hold values from 0 to 127; in each aligned block of 128 rows (0 to 127, 128 to 255, ..., all dimensions but the last counted through in order) at most 2 rows name the same one
Outputs:
- child_rows: float32 [32768, 1024], P(('rows', 'cols'))
Inputs may be any that keep to these rules, and one draw needn't show every extreme that they name: `owner_map`: among the rows of one device (one index of the first dimension), no owner is named more than 2 times, a bound that some block reaches; every owner is named somewhere.
All inputs are finite; a program needn't handle non-finite values.
Results may differ from a plain program's by a relative error of at most 0.008.
Values may be sent and summed in bfloat16 or wider, within the bound.
No kernel may reach another device: no remote copies, remote signals or barrier semaphores. Data moves between devices by JAX's collectives and lax.ppermute only.
A program may use at most 64 MiB of HBM per device.

v0:
```python
import jax
import jax.numpy as jnp
from jax import lax
from jax.sharding import PartitionSpec as P


def pair_slot(later, earlier):
    return later * (later - 1) // 2 + earlier


def pack_rows(rows_here, owners, devices, most):
    onehot = (owners[:, None] == jnp.arange(devices, dtype=jnp.int32)[None, :]).astype(jnp.int32)
    ranks = jnp.cumsum(onehot, axis=0) - onehot
    slots = jnp.sum(ranks * onehot, axis=1)
    target = owners * most + slots
    select = (jnp.arange(devices * most, dtype=jnp.int32)[:, None] == target[None, :]).astype(
        jnp.float32
    )
    return jnp.dot(
        select, rows_here, precision=lax.Precision.HIGHEST, preferred_element_type=jnp.float32
    )


def tile_term(tile, vectors):
    return lax.dot_general(
        tile, vectors, (((0,), (0,)), ((), ())), preferred_element_type=jnp.float32
    )


def local(pivot_rhs, bound_sol, border_tiles, lower_tiles, inverse_diag, owner_map):
    devices = lax.axis_size("rows") * lax.axis_size("cols")
    blocks = pivot_rhs.shape[0]
    width_here = pivot_rhs.shape[1]
    sources = pivot_rhs.shape[2]
    rows_dev = owner_map.shape[1]
    most = max(2, 2 * rows_dev // devices)
    border_part = lax.dot_general(
        border_tiles, bound_sol, (((0,), (0,)), ((), ())), preferred_element_type=jnp.float32
    )
    pending = []
    border_full = lax.psum(border_part, "rows")
    for k in range(blocks):
        pending.append(jnp.zeros((width_here, sources), jnp.float32))
    rounded = [None] * blocks
    own_rows = [None] * blocks
    for k in reversed(range(blocks)):
        local_sum = pending[k]
        for j in range(k + 1, blocks):
            local_sum = local_sum + tile_term(lower_tiles[pair_slot(j, k)], rounded[j])
        summed = lax.psum(local_sum, "rows")
        summed = summed + border_full[k]
        residual = (pivot_rhs[k] - summed).astype(jnp.bfloat16)
        inverse_here = inverse_diag[k]
        solved_here = lax.psum_scatter(
            tile_term(inverse_here, residual), "cols", scatter_dimension=0, tiled=True
        )
        own_rows[k] = solved_here
        if k > 0:
            rounded[k] = lax.all_gather(
                solved_here.astype(jnp.bfloat16), "cols", axis=0, tiled=True
            )
    rows_here = jnp.concatenate(own_rows, axis=0)
    owners = owner_map[0, :, 0]
    buffer = pack_rows(rows_here, owners, devices, most).reshape(devices, most, sources)
    received = lax.all_to_all(buffer, ("rows", "cols"), split_axis=0, concat_axis=0, tiled=True)
    return received.reshape(devices * most, sources)


def solution(mesh):
    placed = (
        P(None, "cols", None),
        P("rows", None),
        P("rows", None, "cols"),
        P(None, "rows", "cols"),
        P(None, "cols", "rows"),
        P(("rows", "cols"), None, None),
    )
    return jax.shard_map(
        local, mesh=mesh, in_specs=placed, out_specs=P(("rows", "cols"), None), check_vma=False
    )
```

profile of v0, /device:TPU:1, one launch (start us, length us, event | category | flops | bytes accessed | tf_op | source)
XLA Modules:
  0.0 773.4 jit_solution(16388644528442897463)
XLA Ops:
  6.5 10.0 %fusion = f32[4,256,1024]{2,1,0:T(8,128)} fusion(bf16[2048,1024]{1,0:T(8,128)(2,1)} %param.7, bf16[2048,4,256]{2,1,0:T(4,128)(2,1)} %param.8), kind=kOutput, calls=%fused_computation | convolution fusion | flops 4294967296 | bytes 12582912 | tf_op jit(solution)/shard_map/dot_general | solution.py:37
  16.6 74.5 %all-reduce.5.cloned.1.call-done = f32[4,256,1024]{2,1,0:T(8,128)} async-done(((f32[4,256,1024]{2,1,0:T(8,128)}), f32[4,256,1024]{2,1,0:T(8,128)}) %all-reduce.5.cloned.1.call-update) | async-done | bytes 4194320 | tf_op jit(solution)/shard_map/psum | solution.py:41
  91.2 2.1 convolution_bitcast_fusion.3
  93.2 1.8 copy.28
  95.1 74.3 %reduce-scatter.13.cloned.1.call-done = f32[32,1024]{1,0:T(8,128)} async-done(((f32[512,1024]{1,0:T(8,128)}), f32[32,1024]{1,0:T(8,128)}) %reduce-scatter.13.cloned.1.call-update) | async-done | bytes 131088 | tf_op jit(solution)/shard_map/reduce_scatter | solution.py:54
  171.1 42.9 %all-gather.4.cloned.1.call-done = bf16[512,1024]{1,0:T(8,128)(2,1)} async-done(((bf16[32,1024]{1,0:T(8,128)(2,1)}), bf16[512,1024]{1,0:T(8,128)(2,1)}) %all-gather.4.cloned.1.call-update) | async-done | bytes 1048592 | tf_op jit(solution)/shard_map/all_gather | solution.py:59
  214.0 2.7 convolution_bitcast_fusion.4
  216.8 61.5 %all-reduce.7.cloned.1.call-done = f32[256,1024]{1,0:T(8,128)} async-done(((f32[256,1024]{1,0:T(8,128)}), f32[256,1024]{1,0:T(8,128)}) %all-reduce.7.cloned.1.call-update) | async-done | bytes 1048592 | tf_op jit(solution)/shard_map/psum | solution.py:50
  278.3 2.5 convolution_bitcast_fusion.2
  280.8 1.8 copy.30
  282.7 73.8 %reduce-scatter.15.cloned.1.call-done = f32[32,1024]{1,0:T(8,128)} async-done(((f32[512,1024]{1,0:T(8,128)}), f32[32,1024]{1,0:T(8,128)}) %reduce-scatter.15.cloned.1.call-update) | async-done | bytes 131088 | tf_op jit(solution)/shard_map/reduce_scatter | solution.py:54
  358.1 42.5 %all-gather.6.cloned.1.call-done = bf16[512,1024]{1,0:T(8,128)(2,1)} async-done(((bf16[32,1024]{1,0:T(8,128)(2,1)}), bf16[512,1024]{1,0:T(8,128)(2,1)}) %all-gather.6.cloned.1.call-update) | async-done | bytes 1048592 | tf_op jit(solution)/shard_map/all_gather | solution.py:59
  402.4 2.4 fusion.4
  404.9 61.5 %all-reduce.9.cloned.1.call-done = f32[256,1024]{1,0:T(8,128)} async-done(((f32[256,1024]{1,0:T(8,128)}), f32[256,1024]{1,0:T(8,128)}) %all-reduce.9.cloned.1.call-update) | async-done | bytes 1048592 | tf_op jit(solution)/shard_map/psum | solution.py:50
  466.4 2.5 convolution_bitcast_fusion.1
  468.8 1.8 copy.32
  470.8 73.8 %reduce-scatter.17.cloned.1.call-done = f32[32,1024]{1,0:T(8,128)} async-done(((f32[512,1024]{1,0:T(8,128)}), f32[32,1024]{1,0:T(8,128)}) %reduce-scatter.17.cloned.1.call-update) | async-done | bytes 131088 | tf_op jit(solution)/shard_map/reduce_scatter | solution.py:54
  546.2 42.9 %all-gather.8.cloned.1.call-done = bf16[512,1024]{1,0:T(8,128)(2,1)} async-done(((bf16[32,1024]{1,0:T(8,128)(2,1)}), bf16[512,1024]{1,0:T(8,128)(2,1)}) %all-gather.8.cloned.1.call-update) | async-done | bytes 1048592 | tf_op jit(solution)/shard_map/all_gather | solution.py:59
  592.3 2.4 fusion.3
  595.0 61.3 %all-reduce.11.cloned.1.call-done = f32[256,1024]{1,0:T(8,128)} async-done(((f32[256,1024]{1,0:T(8,128)}), f32[256,1024]{1,0:T(8,128)}) %all-reduce.11.cloned.1.call-update) | async-done | bytes 1048592 | tf_op jit(solution)/shard_map/psum | solution.py:50
  656.3 2.5 convolution_bitcast_fusion
  658.8 1.9 copy.34
  661.8 72.8 %reduce-scatter.19.cloned.1.call-done = f32[32,1024]{1,0:T(8,128)} async-done(((f32[512,1024]{1,0:T(8,128)}), f32[32,1024]{1,0:T(8,128)}) %reduce-scatter.19.cloned.1.call-update) | async-done | bytes 131088
  737.3 27.9 %all_to_all.5 = f32[128,2,1024]{2,1,0:T(2,128)S(1)} all-to-all(f32[128,2,1024]{2,1,0:T(2,128)S(1)} %reshape.16), channel_id=1, replica_groups=mesh['rows'=8,'cols'=16] {'rows','cols'}, dimensions={0} | all-to-all | bytes 2097152 | tf_op jit(solution)/shard_map/all_to_all | solution.py:65
  (51 shorter events, 15.8 us)
Async XLA Ops:
  6.5 84.6 %all-reduce.5.cloned.1.call-start = ((), (), s32[]{:S(2)}) async-start(), calls=%async_computation.5 | async-start | bytes 8388608 | tf_op jit(solution)/shard_map/psum | solution.py:41
  16.6 152.9 %reduce-scatter.13.cloned.1.call-start = ((), (), s32[]{:S(2)}) async-start(), calls=%async_computation.12 | async-start | bytes 2228224 | tf_op jit(solution)/shard_map/reduce_scatter | solution.py:54
  95.1 118.9 %all-gather.4.cloned.1.call-start = ((), (), s32[]{:S(2)}) async-start(), calls=%async_computation.6 | async-start | bytes 1114112 | tf_op jit(solution)/shard_map/all_gather | solution.py:59
  171.0 107.3 %all-reduce.7.cloned.1.call-start = ((), (), s32[]{:S(2)}) async-start(), calls=%async_computation.7 | async-start | bytes 2097152 | tf_op jit(solution)/shard_map/psum | solution.py:50
  216.7 139.7 %reduce-scatter.15.cloned.1.call-start = ((), (), s32[]{:S(2)}) async-start(), calls=%async_computation.13 | async-start | bytes 2228224 | tf_op jit(solution)/shard_map/reduce_scatter | solution.py:54
  280.8 121.6 %copy-start = (bf16[512,1024]{1,0:T(8,128)(2,1)S(1)}, bf16[512,1024]{1,0:T(8,128)(2,1)}, u32[]{:S(2)}) copy-start(bf16[512,1024]{1,0:T(8,128)(2,1)} %all-gather.4.cloned.1.call-done) | copy-start | bytes 3145732
  282.6 118.0 %all-gather.6.cloned.1.call-start = ((), (), s32[]{:S(2)}) async-start(), calls=%async_computation.8 | async-start | bytes 1114112 | tf_op jit(solution)/shard_map/all_gather | solution.py:59
  358.0 108.3 %all-reduce.9.cloned.1.call-start = ((), (), s32[]{:S(2)}) async-start(), calls=%async_computation.9 | async-start | bytes 2097152 | tf_op jit(solution)/shard_map/psum | solution.py:50
  404.8 139.7 %reduce-scatter.17.cloned.1.call-start = ((), (), s32[]{:S(2)}) async-start(), calls=%async_computation.14 | async-start | bytes 2228224 | tf_op jit(solution)/shard_map/reduce_scatter | solution.py:54
  470.7 120.1 %copy-start.1 = (bf16[512,1024]{1,0:T(8,128)(2,1)S(1)}, bf16[512,1024]{1,0:T(8,128)(2,1)}, u32[]{:S(2)}) copy-start(bf16[512,1024]{1,0:T(8,128)(2,1)} %all-gather.6.cloned.1.call-done) | copy-start | bytes 3145732
  470.7 118.4 %all-gather.8.cloned.1.call-start = ((), (), s32[]{:S(2)}) async-start(), calls=%async_computation.10 | async-start | bytes 1114112 | tf_op jit(solution)/shard_map/all_gather | solution.py:59
  546.1 110.1 %all-reduce.11.cloned.1.call-start = ((), (), s32[]{:S(2)}) async-start(), calls=%async_computation.11 | async-start | bytes 2097152 | tf_op jit(solution)/shard_map/psum | solution.py:50
  594.7 139.9 %reduce-scatter.19.cloned.1.call-start = ((), (), s32[]{:S(2)}) async-start(), calls=%async_computation.15 | async-start | bytes 2228224
  658.8 1.9 copy-start.5
  658.8 2.4 copy-start.2
  658.8 2.6 copy-start.3
  658.8 2.8 copy-start.4
Sparse Core Ops, SparseCore 0:
  16.7 74.4 all-reduce.4
  95.2 74.1 reduce-scatter.12
  171.8 42.1 all-gather.3
  216.9 61.3 all-reduce.6
  282.8 73.6 reduce-scatter.14
  358.5 42.1 all-gather.5
  404.9 61.3 all-reduce.8
  470.8 73.6 reduce-scatter.16
  546.9 42.0 all-gather.7
  594.8 61.3 all-reduce.10
  660.8 73.7 reduce-scatter.18
where the time goes:
time: 774 us; the launch traced here: 773 us
  waiting for transfers between devices  682 us (88%)
  matrix products  33 us (4%)
  blocking collectives  27.9 us (4%)
  between operations  13.4 us (2%)
  local copies, waits for them, and re-layouts  11.4 us (1%)
    reduce_scatter x3, waiting for transfers between devices, local(): lax.psum_scatter(tile_term(inverse_here, residual), 'cols', scatter_dimen...  222 us
    psum x3, waiting for transfers between devices, local(): summed = lax.psum(local_sum, 'rows')  184 us
    all_gather x3, waiting for transfers between devices, local(): lax.all_gather(solved_here.astype(jnp.bfloat16), 'cols', axis=0, tiled=True)  128 us
    psum x1, waiting for transfers between devices, local(): border_full = lax.psum(border_part, 'rows')  74.5 us
    unnamed x12, waiting for transfers between devices  73 us
    all_to_all x1, blocking collectives, local(): lax.all_to_all(buffer, ('rows', 'cols'), split_axis=0, concat_axis=0, til...  27.9 us
    dot_general x10, matrix products, tile_term(): lax.dot_general(tile, vectors, (((0,), (0,)), ((), ())), preferred_elemen...  22 us
  transfers between devices with their start and end apart: 11, of which 11 were waited for; matrix products, arithmetic and copies ran while one was open for 0% of the time, Pallas kernels for 0%

commit v1 on v0

--- a/solution.py
+++ b/solution.py
@@ -1,7 +1,37 @@
+import functools
 import jax
 import jax.numpy as jnp
 from jax import lax
 from jax.sharding import PartitionSpec as P
+
+
+def enter_the_loops(inner_x, along_dim):
+    before = list(inner_x.shape[1:])
+    before[along_dim] *= inner_x.shape[0]
+    return jnp.moveaxis(inner_x, 0, along_dim).reshape(before)
+
+
+def prepare_the_leaf(piece_in, link_axis, k_dim):
+    many = jax.lax.axis_size(link_axis)
+    frames = list(map(lambda rr: (rr, (rr + 1) % many), range(many)))
+    rows = [(jj, ix) for ix, jj in frames]
+    block_last, s_next = ([], [])
+    at = 0
+    while at < many - 1:
+        if at % 2 == 0:
+            block_last.append(
+                jax.lax.ppermute(block_last[-1] if block_last else piece_in, link_axis, frames)
+            )
+        else:
+            s_next.append(jax.lax.ppermute(s_next[-1] if s_next else piece_in, link_axis, rows))
+        at += 1
+    raw_out = jnp.stack([*block_last[::-1], piece_in, *s_next], 0)
+    vec_out = jax.lax.axis_index(link_axis) - len(block_last)
+    raw_out = raw_out[(jnp.arange(many) - vec_out) % many]
+    return enter_the_loops(raw_out, k_dim)
+
+
+_advance_sites = functools.partial(prepare_the_leaf, link_axis="cols", k_dim=0)
 
 
 def pair_slot(later, earlier):
@@ -56,9 +86,7 @@
         )
         own_rows[k] = solved_here
         if k > 0:
-            rounded[k] = lax.all_gather(
-                solved_here.astype(jnp.bfloat16), "cols", axis=0, tiled=True
-            )
+            rounded[k] = _advance_sites(solved_here.astype(jnp.bfloat16))
     rows_here = jnp.concatenate(own_rows, axis=0)
     owners = owner_map[0, :, 0]
     buffer = pack_rows(rows_here, owners, devices, most).reshape(devices, most, sources)

time: 774 us -> 939 us (1.21)
  starting transfers between devices: 0.6 us -> 113 us
  local copies, waits for them, and re-layouts: 11.4 us -> 65.8 us
    reduce_scatter x3 -> x0, waiting for transfers between devices: 222 us -> none  [local(): lax.psum_scatter(tile_term(inverse_here, residual), 'cols', scatter_dimen...]
    unnamed x12, waiting for transfers between devices: 73 us -> 286 us
    all_gather x3 -> x0, waiting for transfers between devices: 128 us -> none  [local(): lax.all_gather(solved_here.astype(jnp.bfloat16), 'cols', axis=0, tiled=True)]
    ppermute x0 -> x45, starting transfers between devices: none -> 104 us  [the longest x21 101 us: prepare_the_leaf(): jax.lax.ppermute(s_next[-1] if s_next else piece_in, link_axis, rows)]
    ppermute x0 -> x45, waiting for transfers between devices: none -> 98.9 us  [the longest x24 98.5 us: prepare_the_leaf(): jax.lax.ppermute(block_last[-1] if block_last else piece_in, link_axis, f...]
    another operation x0 -> x51, local copies, waits for them, and re-layouts: none -> 34.3 us  [prepare_the_leaf(): raw_out = jnp.stack([*block_last[::-1], piece_in, *s_next], 0)]
    psum x3, waiting for transfers between devices: 184 us -> 214 us  [local(): summed = lax.psum(local_sum, 'rows')]
    unnamed x20 -> x95, local copies, waits for them, and re-layouts: 9.1 us -> 26.1 us
  transfers between devices with their start and end apart: 11 -> 53, of which waited for: 11 -> 34; matrix products, arithmetic and copies ran while one was open for 0% -> 3% of each run, Pallas kernels for 0% -> 0%
where the time goes in v1:
time: 939 us; the launch traced here: 930 us
  waiting for transfers between devices  674 us (72%)
  starting transfers between devices  113 us (12%)
  local copies, waits for them, and re-layouts  65.8 us (7%)
  matrix products  34.5 us (4%)
  blocking collectives  27.9 us (3%)
  between operations  14.4 us (2%)
    unnamed x12, waiting for transfers between devices  286 us
    psum x3, waiting for transfers between devices, local(): summed = lax.psum(local_sum, 'rows')  214 us
    ppermute x21, starting transfers between devices, prepare_the_leaf(): jax.lax.ppermute(s_next[-1] if s_next else piece_in, link_axis, rows)  101 us
    ppermute x24, waiting for transfers between devices, prepare_the_leaf(): jax.lax.ppermute(block_last[-1] if block_last else piece_in, link_axis, f...  98.5 us
    psum x1, waiting for transfers between devices, local(): border_full = lax.psum(border_part, 'rows')  74.5 us
    another operation x51, local copies, waits for them, and re-layouts, prepare_the_leaf(): raw_out = jnp.stack([*block_last[::-1], piece_in, *s_next], 0)  34.3 us
    all_to_all x1, blocking collectives, local(): lax.all_to_all(buffer, ('rows', 'cols'), split_axis=0, concat_axis=0, til...  27.9 us
    unnamed x95, local copies, waits for them, and re-layouts  26.1 us
  transfers between devices with their start and end apart: 53, of which 34 were waited for; matrix products, arithmetic and copies ran while one was open for 3% of the time, Pallas kernels for 0%

profile of v1, /device:TPU:1, one launch (start us, length us, event | category | flops | bytes accessed | tf_op | source)
XLA Modules:
  0.0 930.0 jit_solution(9254737905798921465)
XLA Ops:
  6.5 10.0 %fusion = f32[4,256,1024]{2,1,0:T(8,128)} fusion(bf16[2048,1024]{1,0:T(8,128)(2,1)} %param.7, bf16[2048,4,256]{2,1,0:T(4,128)(2,1)} %param.8), kind=kOutput, calls=%fused_computation.3 | convolution fusion | flops 4294967296 | bytes 12582912 | tf_op jit(solution)/shard_map/dot_general | solution.py:67
  16.6 74.5 %all-reduce.5.cloned.1.call-done = f32[4,256,1024]{2,1,0:T(8,128)} async-done(((f32[4,256,1024]{2,1,0:T(8,128)}), f32[4,256,1024]{2,1,0:T(8,128)}) %all-reduce.5.cloned.1.call-update) | async-done | bytes 4194320 | tf_op jit(solution)/shard_map/psum | solution.py:71
  95.2 74.3 %reduce-scatter.13.cloned.1.call-done = f32[32,1024]{1,0:T(8,128)} async-done(((f32[512,1024]{1,0:T(8,128)}), f32[32,1024]{1,0:T(8,128)}) %reduce-scatter.13.cloned.1.call-update) | async-done | bytes 131088
  213.9 5.0 collective-permute-start.13
  219.0 5.1 collective-permute-done.5
  224.2 5.3 collective-permute-start.14
  229.5 6.0 collective-permute-done.6
  241.5 6.0 collective-permute-done.7
  251.9 68.0 %all-reduce.7.cloned.1.call-done = f32[256,1024]{1,0:T(8,128)} async-done(((f32[256,1024]{1,0:T(8,128)}), f32[256,1024]{1,0:T(8,128)}) %all-reduce.7.cloned.1.call-update) | async-done | bytes 1048592 | tf_op jit(solution)/shard_map/psum | solution.py:80
  324.3 73.8 %reduce-scatter.15.cloned.1.call-done = f32[32,1024]{1,0:T(8,128)} async-done(((f32[512,1024]{1,0:T(8,128)}), f32[32,1024]{1,0:T(8,128)}) %reduce-scatter.15.cloned.1.call-update) | async-done | bytes 131088
  442.6 5.1 collective-permute-start.28
  447.6 5.1 collective-permute-done.20
  452.8 5.3 collective-permute-start.29
  458.2 6.0 collective-permute-done.21
  483.9 72.3 %all-reduce.9.cloned.1.call-done = f32[256,1024]{1,0:T(8,128)} async-done(((f32[256,1024]{1,0:T(8,128)}), f32[256,1024]{1,0:T(8,128)}) %all-reduce.9.cloned.1.call-update) | async-done | bytes 1048592 | tf_op jit(solution)/shard_map/psum | solution.py:80
  563.0 9.3 %all-reduce.11.cloned.1.call-start = ((), (), s32[]{:S(2)}) async-start(), calls=%async_computation.8 | async-start | bytes 2097152 | tf_op jit(solution)/shard_map/psum | solution.py:80
  572.4 64.5 %reduce-scatter.17.cloned.1.call-done = f32[32,1024]{1,0:T(8,128)} async-done(((f32[512,1024]{1,0:T(8,128)}), f32[32,1024]{1,0:T(8,128)}) %reduce-scatter.17.cloned.1.call-update) | async-done | bytes 131088
  681.4 5.1 collective-permute-start.43
  686.5 5.1 collective-permute-done.35
  691.7 5.3 collective-permute-start.44
  697.0 6.0 collective-permute-done.36
  737.7 73.8 %all-reduce.11.cloned.1.call-done = f32[256,1024]{1,0:T(8,128)} async-done(((f32[256,1024]{1,0:T(8,128)}), f32[256,1024]{1,0:T(8,128)}) %all-reduce.11.cloned.1.call-update) | async-done | bytes 1048592 | tf_op jit(solution)/shard_map/psum | solution.py:80
  816.4 73.5 %reduce-scatter.19.cloned.1.call-done = f32[32,1024]{1,0:T(8,128)} async-done(((f32[512,1024]{1,0:T(8,128)}), f32[32,1024]{1,0:T(8,128)}) %reduce-scatter.19.cloned.1.call-update) | async-done | bytes 131088
  893.6 27.9 %all_to_all.5 = f32[128,2,1024]{2,1,0:T(2,128)S(1)} all-to-all(f32[128,2,1024]{2,1,0:T(2,128)S(1)} %reshape.77), channel_id=1, replica_groups=mesh['rows'=8,'cols'=16] {'rows','cols'}, dimensions={0} | all-to-all | bytes 2097152 | tf_op jit(solution)/shard_map/all_to_all | solution.py:93
  (266 shorter events, 223.3 us)
Async XLA Ops:
  6.5 84.6 %all-reduce.5.cloned.1.call-start = ((), (), s32[]{:S(2)}) async-start(), calls=%async_computation.5 | async-start | bytes 8388608 | tf_op jit(solution)/shard_map/psum | solution.py:71
  16.6 152.9 %reduce-scatter.13.cloned.1.call-start = ((), (), s32[]{:S(2)}) async-start(), calls=%async_computation.9 | async-start | bytes 2228224
  95.1 224.7 %all-reduce.7.cloned.1.call-start = ((), (), s32[]{:S(2)}) async-start(), calls=%async_computation.6 | async-start | bytes 2097152 | tf_op jit(solution)/shard_map/psum | solution.py:80
  204.9 9.1 collective-permute-start.12
  213.9 10.1 %collective-permute-start.5 = (bf16[32,1024]{0,1:T(8,128)(2,1)S(1)}, bf16[32,1024]{0,1:T(8,128)(2,1)S(1)}, u32[]{:S(2)}, u32[]{:S(2)}) collective-permute-start(bf16[32,1024]{0,1:T(8,128)(2,1)S(1)} %collective-permute-done.4), channel_id=1, source_target_pairs={{0,1},{1,2},{2,3},{3,4},{4,5},{5,6},{6,7},{7,8},{8,9},{9,10},{10,1... | collective-permute-start | bytes 196616 | tf_op jit(solution)/shard_map/ppermute | solution.py:23
  213.9 10.2 %collective-permute-start.13 = (bf16[32,1024]{0,1:T(8,128)(2,1)S(1)}, bf16[32,1024]{0,1:T(8,128)(2,1)}, u32[]{:S(2)}, u32[]{:S(2)}) collective-permute-start(bf16[32,1024]{0,1:T(8,128)(2,1)S(1)} %collective-permute-done.12), channel_id=1, source_target_pairs={{1,0},{2,1},{3,2},{4,3},{5,4},{6,5},{7,6},{8,7},{9,8},{10,9},{11,1... | collective-permute-start | bytes 196616 | tf_op jit(solution)/shard_map/ppermute | solution.py:26
  224.1 11.5 %collective-permute-start.6 = (bf16[32,1024]{0,1:T(8,128)(2,1)S(1)}, bf16[32,1024]{0,1:T(8,128)(2,1)}, u32[]{:S(2)}, u32[]{:S(2)}) collective-permute-start(bf16[32,1024]{0,1:T(8,128)(2,1)S(1)} %collective-permute-done.5), channel_id=1, source_target_pairs={{0,1},{1,2},{2,3},{3,4},{4,5},{5,6},{6,7},{7,8},{8,9},{9,10},{10,1... | collective-permute-start | bytes 196616 | tf_op jit(solution)/shard_map/ppermute | solution.py:23
  224.2 15.2 %collective-permute-start.14 = (bf16[32,1024]{0,1:T(8,128)(2,1)}, bf16[32,1024]{0,1:T(8,128)(2,1)}, u32[]{:S(2)}, u32[]{:S(2)}) collective-permute-start(bf16[32,1024]{0,1:T(8,128)(2,1)} %collective-permute-done.13), channel_id=1, source_target_pairs={{1,0},{2,1},{3,2},{4,3},{5,4},{6,5},{7,6},{8,7},{9,8},{10,9},{11,1... | collective-permute-start | bytes 196616 | tf_op jit(solution)/shard_map/ppermute | solution.py:26
  235.5 11.9 %collective-permute-start.7 = (bf16[32,1024]{0,1:T(8,128)(2,1)}, bf16[32,1024]{0,1:T(8,128)(2,1)}, u32[]{:S(2)}, u32[]{:S(2)}) collective-permute-start(bf16[32,1024]{0,1:T(8,128)(2,1)} %collective-permute-done.6), channel_id=1, source_target_pairs={{0,1},{1,2},{2,3},{3,4},{4,5},{5,6},{6,7},{7,8},{8,9},{9,10},{10,1... | collective-permute-start | bytes 196616 | tf_op jit(solution)/shard_map/ppermute | solution.py:23
  251.9 146.3 %reduce-scatter.15.cloned.1.call-start = ((), (), s32[]{:S(2)}) async-start(), calls=%async_computation.10 | async-start | bytes 2228224
  324.2 232.0 %all-reduce.9.cloned.1.call-start = ((), (), s32[]{:S(2)}) async-start(), calls=%async_computation.7 | async-start | bytes 2097152 | tf_op jit(solution)/shard_map/psum | solution.py:80
  442.6 10.1 %collective-permute-start.20 = (bf16[32,1024]{0,1:T(8,128)(2,1)S(1)}, bf16[32,1024]{0,1:T(8,128)(2,1)S(1)}, u32[]{:S(2)}, u32[]{:S(2)}) collective-permute-start(bf16[32,1024]{0,1:T(8,128)(2,1)S(1)} %collective-permute-done.19), channel_id=1, source_target_pairs={{0,1},{1,2},{2,3},{3,4},{4,5},{5,6},{6,7},{7,8},{8,9},{9,10},{10,1... | collective-permute-start | bytes 196616 | tf_op jit(solution)/shard_map/ppermute | solution.py:23
  442.6 10.2 %collective-permute-start.28 = (bf16[32,1024]{0,1:T(8,128)(2,1)S(1)}, bf16[32,1024]{0,1:T(8,128)(2,1)}, u32[]{:S(2)}, u32[]{:S(2)}) collective-permute-start(bf16[32,1024]{0,1:T(8,128)(2,1)S(1)} %collective-permute-done.27), channel_id=1, source_target_pairs={{1,0},{2,1},{3,2},{4,3},{5,4},{6,5},{7,6},{8,7},{9,8},{10,9},{11,1... | collective-permute-start | bytes 196616 | tf_op jit(solution)/shard_map/ppermute | solution.py:26
  452.7 11.5 %collective-permute-start.21 = (bf16[32,1024]{0,1:T(8,128)(2,1)S(1)}, bf16[32,1024]{0,1:T(8,128)(2,1)}, u32[]{:S(2)}, u32[]{:S(2)}) collective-permute-start(bf16[32,1024]{0,1:T(8,128)(2,1)S(1)} %collective-permute-done.20), channel_id=1, source_target_pairs={{0,1},{1,2},{2,3},{3,4},{4,5},{5,6},{6,7},{7,8},{8,9},{9,10},{10,1... | collective-permute-start | bytes 196616 | tf_op jit(solution)/shard_map/ppermute | solution.py:23
  452.8 18.8 %collective-permute-start.29 = (bf16[32,1024]{0,1:T(8,128)(2,1)}, bf16[32,1024]{0,1:T(8,128)(2,1)}, u32[]{:S(2)}, u32[]{:S(2)}) collective-permute-start(bf16[32,1024]{0,1:T(8,128)(2,1)} %collective-permute-done.28), channel_id=1, source_target_pairs={{1,0},{2,1},{3,2},{4,3},{5,4},{6,5},{7,6},{8,7},{9,8},{10,9},{11,1... | collective-permute-start | bytes 196616 | tf_op jit(solution)/shard_map/ppermute | solution.py:26
  464.2 11.5 %collective-permute-start.22 = (bf16[32,1024]{0,1:T(8,128)(2,1)}, bf16[32,1024]{0,1:T(8,128)(2,1)}, u32[]{:S(2)}, u32[]{:S(2)}) collective-permute-start(bf16[32,1024]{0,1:T(8,128)(2,1)} %collective-permute-done.21), channel_id=1, source_target_pairs={{0,1},{1,2},{2,3},{3,4},{4,5},{5,6},{6,7},{7,8},{8,9},{9,10},{10,1... | collective-permute-start | bytes 196616 | tf_op jit(solution)/shard_map/ppermute | solution.py:23
  483.8 153.1 %reduce-scatter.17.cloned.1.call-start = ((), (), s32[]{:S(2)}) async-start(), calls=%async_computation.11 | async-start | bytes 2228224
  563.0 248.5 %all-reduce.11.cloned.1.call-start = ((), (), s32[]{:S(2)}) async-start(), calls=%async_computation.8 | async-start | bytes 2097152 | tf_op jit(solution)/shard_map/psum | solution.py:80
  681.4 10.1 %collective-permute-start.35 = (bf16[32,1024]{0,1:T(8,128)(2,1)S(1)}, bf16[32,1024]{0,1:T(8,128)(2,1)S(1)}, u32[]{:S(2)}, u32[]{:S(2)}) collective-permute-start(bf16[32,1024]{0,1:T(8,128)(2,1)S(1)} %collective-permute-done.34), channel_id=1, source_target_pairs={{0,1},{1,2},{2,3},{3,4},{4,5},{5,6},{6,7},{7,8},{8,9},{9,10},{10,1... | collective-permute-start | bytes 196616 | tf_op jit(solution)/shard_map/ppermute | solution.py:23
  681.4 10.2 %collective-permute-start.43 = (bf16[32,1024]{0,1:T(8,128)(2,1)S(1)}, bf16[32,1024]{0,1:T(8,128)(2,1)}, u32[]{:S(2)}, u32[]{:S(2)}) collective-permute-start(bf16[32,1024]{0,1:T(8,128)(2,1)S(1)} %collective-permute-done.42), channel_id=1, source_target_pairs={{1,0},{2,1},{3,2},{4,3},{5,4},{6,5},{7,6},{8,7},{9,8},{10,9},{11,1... | collective-permute-start | bytes 196616 | tf_op jit(solution)/shard_map/ppermute | solution.py:26
  691.5 11.5 %collective-permute-start.36 = (bf16[32,1024]{0,1:T(8,128)(2,1)S(1)}, bf16[32,1024]{0,1:T(8,128)(2,1)}, u32[]{:S(2)}, u32[]{:S(2)}) collective-permute-start(bf16[32,1024]{0,1:T(8,128)(2,1)S(1)} %collective-permute-done.35), channel_id=1, source_target_pairs={{0,1},{1,2},{2,3},{3,4},{4,5},{5,6},{6,7},{7,8},{8,9},{9,10},{10,1... | collective-permute-start | bytes 196616 | tf_op jit(solution)/shard_map/ppermute | solution.py:23
  691.7 22.6 %collective-permute-start.44 = (bf16[32,1024]{0,1:T(8,128)(2,1)}, bf16[32,1024]{0,1:T(8,128)(2,1)}, u32[]{:S(2)}, u32[]{:S(2)}) collective-permute-start(bf16[32,1024]{0,1:T(8,128)(2,1)} %collective-permute-done.43), channel_id=1, source_target_pairs={{1,0},{2,1},{3,2},{4,3},{5,4},{6,5},{7,6},{8,7},{9,8},{10,9},{11,1... | collective-permute-start | bytes 196616 | tf_op jit(solution)/shard_map/ppermute | solution.py:26
  703.1 13.9 %collective-permute-start.37 = (bf16[32,1024]{0,1:T(8,128)(2,1)}, bf16[32,1024]{0,1:T(8,128)(2,1)}, u32[]{:S(2)}, u32[]{:S(2)}) collective-permute-start(bf16[32,1024]{0,1:T(8,128)(2,1)} %collective-permute-done.36), channel_id=1, source_target_pairs={{0,1},{1,2},{2,3},{3,4},{4,5},{5,6},{6,7},{7,8},{8,9},{9,10},{10,1... | collective-permute-start | bytes 196616 | tf_op jit(solution)/shard_map/ppermute | solution.py:23
  737.7 152.2 %reduce-scatter.19.cloned.1.call-start = ((), (), s32[]{:S(2)}) async-start(), calls=%async_computation.12 | async-start | bytes 2228224
  (50 other events, 1070.8 us)
Sparse Core Ops, SparseCore 0:
  16.7 74.4 all-reduce.4
  95.2 74.1 reduce-scatter.12
  252.0 67.8 all-reduce.6
  324.3 73.7 reduce-scatter.14
  484.0 72.1 all-reduce.8
  563.2 73.7 reduce-scatter.16
  737.8 73.6 all-reduce.10
  816.0 73.7 reduce-scatter.18
